TPU v7x, 32 devices: a whole 2x2x4 slice. The times are simulated.
32 devices in a mesh: hi: 4 (over y, x), lo: 8 (over z, core).
Axes of the slice: x: 2, y: 2, z: 4, core: 2. Of those that a mesh axis runs over, the one named last changes fastest.
Arguments:
- initial_state: float32 [2, 4194304], P(None, ('hi', 'lo')), may hold values from -60 to 60
- gate_angles: float32 [2, 3, 22], replicated, may hold values from -3.140625 to 3.140625
- damp_qubits: int32 [2, 4], replicated, may hold values from 0 to 16, as said below
- kraus_branch: int32 [2, 4], replicated, may hold values 0 or 1
- damping: float32 [2, 4], replicated, may hold values from 0.1 to 0.6
Outputs:
- final_state: float32 [2, 4194304], P(None, ('hi', 'lo'))
- branch_weights: float32 [2, 4], replicated
Inputs may be any that keep to these rules, and one draw needn't show every extreme that they name: `damp_qubits`: the 8 entries are distinct qubits.
All inputs are finite; a program needn't handle non-finite values.
Results may differ from a plain program's by a relative error of at most 0.00022.
Values sent between devices are 32-bit elements; how exact they have to be, the bound alone decides.
A program may use at most 128 MiB of HBM per device.

v0:
```python
import functools
import heapq

import jax
import jax.numpy as jnp
from jax import lax
from jax.experimental import pallas as pl
from jax.experimental.pallas import tpu as pltpu
from jax.sharding import PartitionSpec as P

epsilon = 1e-06
LANE_BITS = 7
MESH = pl.DeviceIdType.MESH


def gate_entries(angles):
    half_theta = angles[1] * 0.5
    cosine = jnp.cos(half_theta)
    sine = jnp.sin(half_theta)
    summed = (angles[0] + angles[2]) * 0.5
    differ = (angles[0] - angles[2]) * 0.5
    cos_sum, sin_sum = jnp.cos(summed), jnp.sin(summed)
    cos_dif, sin_dif = jnp.cos(differ), jnp.sin(differ)
    real = [cos_sum * cosine, -cos_dif * sine, cos_dif * sine, cos_sum * cosine]
    imag = [-sin_sum * cosine, sin_dif * sine, sin_dif * sine, sin_sum * cosine]
    return (real, imag)


def product(left, right):
    lr, li = left
    rr, ri = right
    real, imag = [], []
    for row in range(2):
        for col in range(2):
            real.append(
                lr[2 * row] * rr[col]
                - li[2 * row] * ri[col]
                + lr[2 * row + 1] * rr[2 + col]
                - li[2 * row + 1] * ri[2 + col]
            )
            imag.append(
                lr[2 * row] * ri[col]
                + li[2 * row] * rr[col]
                + lr[2 * row + 1] * ri[2 + col]
                + li[2 * row + 1] * rr[2 + col]
            )
    return (real, imag)


def real_times(left, right):
    rr, ri = right
    real, imag = [], []
    for row in range(2):
        for col in range(2):
            real.append(left[2 * row] * rr[col] + left[2 * row + 1] * rr[2 + col])
            imag.append(left[2 * row] * ri[col] + left[2 * row + 1] * ri[2 + col])
    return (real, imag)


def kraus_entries(qubits, targets, branches, rates):
    ids = lax.iota(jnp.int32, qubits)
    one = jnp.ones((qubits,), jnp.float32)
    zero = jnp.zeros((qubits,), jnp.float32)
    entries = [one, zero, zero, one]
    for slot in range(targets.shape[0]):
        here = ids == targets[slot]
        jump = branches[slot] == 1
        keep = jnp.sqrt(1.0 - rates[slot])
        drop = jnp.sqrt(rates[slot])
        values = [
            jnp.where(jump, 0.0, 1.0),
            jnp.where(jump, drop, 0.0),
            0.0,
            jnp.where(jump, 0.0, keep),
        ]
        entries = [jnp.where(here, v, e) for v, e in zip(values, entries)]
    return entries


def tables(gate_angles, damp_qubits, kraus_branch, damping):
    layers, _, qubits = gate_angles.shape
    rows = []
    total = None
    for layer in range(layers):
        gates = gate_entries(gate_angles[layer])
        total = gates if total is None else product(gates, total)
        kraus = kraus_entries(qubits, damp_qubits[layer], kraus_branch[layer], damping[layer])
        total = real_times(kraus, total)
        rows += total[0] + total[1]
    return jnp.stack(rows)


def plan(bits, heavy, pieces):
    rest = [b for b in bits if b not in heavy]
    orders = []
    for p in range(pieces):
        flip = p % 2
        if len(heavy) == 2:
            order = [heavy[flip]] + (rest[::-1] if flip else rest) + [heavy[1 - flip]]
        else:
            order = bits[p % len(bits):] + bits[:p % len(bits)]
        orders.append(order)
    free = {b: 0.0 for b in bits}
    events = []
    queue = []

    def launch(p, step, now):
        b = orders[p][step]
        cost = 2.8 if b in heavy else (0.3 if b == 0 else 1.4)
        free[b] = max(free[b], now) + cost
        heapq.heappush(queue, (free[b] + 1.5, p, step))

    for p in range(pieces):
        launch(p, 0, 0.2 * (p // 4))
    while queue:
        now, p, step = heapq.heappop(queue)
        events.append((p, step))
        if step + 1 < len(bits):
            launch(p, step + 1, now)
    return orders, events


def split(values):
    high = values.astype(jnp.bfloat16)
    low = (values - high.astype(jnp.float32)).astype(jnp.bfloat16)
    return high, low


def matmul3(a_high, a_low, b_high, b_low):
    dot = functools.partial(jnp.dot, preferred_element_type=jnp.float32)
    return dot(a_high, b_high) + (dot(a_high, b_low) + dot(a_low, b_high))


def kernel(cfg, tab, damp, x_hbm, out_hbm, info_ref, x_ref, out_ref, planes, topped, stage, recv, mats,
           stats, stat_recv, send_sem, recv_sem, stat_send, stat_got, in_sem, out_sem):
    lo_bits, bits = cfg["lo_bits"], cfg["bits"]
    tiles, pieces, piece_rows = cfg["tiles"], cfg["pieces"], cfg["piece_rows"]
    local_bits, layers, slots = cfg["local_bits"], cfg["layers"], cfg["slots"]
    chunks = tiles // 16
    top_bits = chunks.bit_length() - 1
    orders, events = cfg["orders"], cfg["events"]
    last = 8 * (layers - 1)
    me = {"hi": lax.axis_index("hi"), "lo": lax.axis_index("lo")}

    def partner(b):
        axis, apart = ("lo", 1 << b) if b < lo_bits else ("hi", 1 << (b - lo_bits))
        bit = (me[axis] // apart) % 2
        return bit, {axis: me[axis] + apart * (1 - 2 * bit)}

    where_to = {b: partner(b) for b in bits}

    load = pltpu.make_async_copy(x_hbm, x_ref.at[pl.ds(0, 16 * tiles)], in_sem)
    load.start()
    barrier = pltpu.get_barrier_semaphore()
    for b in bits:
        pl.semaphore_signal(barrier, inc=1, device_id=where_to[b][1], device_id_type=MESH)

    def gate(q):
        return [tab[last + e, q] for e in range(8)]

    def build(first, transposed):
        shape = (128, 128)
        row = lax.broadcasted_iota(jnp.int32, shape, 1 if transposed else 0)
        col = lax.broadcasted_iota(jnp.int32, shape, 0 if transposed else 1)
        re = im = None
        for n in range(LANE_BITS):
            g = gate(first + n)
            rb = (row & (1 << n)) != 0
            cb = (col & (1 << n)) != 0
            er = jnp.where(rb, jnp.where(cb, g[3], g[2]), jnp.where(cb, g[1], g[0]))
            ei = jnp.where(rb, jnp.where(cb, g[7], g[6]), jnp.where(cb, g[5], g[4]))
            if re is None:
                re, im = er, ei
            else:
                re, im = re * er - im * ei, re * ei + im * er
        return re, im

    for slot, transposed in ((0, False), (1, True)):
        re, im = build(LANE_BITS * (1 - slot), transposed)
        sign = -1.0 if transposed else 1.0
        quads = ((re, -sign * im), (sign * im, re))
        for r in range(2):
            for c in range(2):
                high, low = split(quads[r][c])
                at = (pl.ds(128 * r, 128), pl.ds(128 * c, 128))
                mats[(2 * slot,) + at] = high
                mats[(2 * slot + 1,) + at] = low

    top_gates = [gate(2 * LANE_BITS + n) for n in range(top_bits)]

    def top_body(i, acc):
        vals = []
        for c in range(chunks):
            base = pl.multiple_of((c * 16 + i) * 16, 16)
            re = x_ref[pl.ds(base, 8, stride=2), :]
            im = x_ref[pl.ds(base + 1, 8, stride=2), :]
            planes[0, 0, c * 16 + i] = re
            planes[0, 1, c * 16 + i] = im
            acc = acc + (re * re + im * im)
            vals.append((re, im))
        for n in range(top_bits):
            g = top_gates[n]
            new = list(vals)
            for c in range(chunks):
                if c >> n & 1:
                    continue
                d = c | 1 << n
                (ar, ai), (br, bi) = vals[c], vals[d]
                new[c] = (
                    g[0] * ar - g[4] * ai + (g[1] * br - g[5] * bi),
                    g[0] * ai + g[4] * ar + (g[1] * bi + g[5] * br),
                )
                new[d] = (
                    g[2] * ar - g[6] * ai + (g[3] * br - g[7] * bi),
                    g[2] * ai + g[6] * ar + (g[3] * bi + g[7] * br),
                )
            vals = new
        at = pl.ds(pl.multiple_of(i * 8, 8), 8)
        for c in range(chunks):
            topped[c, 0, at, :] = vals[c][0]
            topped[c, 1, at, :] = vals[c][1]
        return acc

    load.wait()
    acc = lax.fori_loop(0, 16, top_body, jnp.zeros((8, 128), jnp.float32))
    stats[0] = jnp.zeros_like(stats[0])
    stats[0, 0:1, :] = jnp.sum(acc, axis=0, keepdims=True)

    pl.semaphore_wait(barrier, len(bits))

    copies = {}
    stores = []

    def launch(p, step):
        b = orders[p][step]
        copy = pltpu.make_async_remote_copy(
            src_ref=stage.at[step, p],
            dst_ref=recv.at[step, p],
            send_sem=send_sem.at[step, p],
            recv_sem=recv_sem.at[step, p],
            device_id=where_to[b][1],
            device_id_type=MESH,
        )
        copy.start()
        copies[p, step] = copy

    per_chunk = 128 // piece_rows
    for pair in range(chunks // 2):
        c, d = 2 * pair, 2 * pair + 1
        x = jnp.concatenate(
            [
                jnp.concatenate([topped[c, 0], topped[d, 0]], axis=1),
                jnp.concatenate([topped[c, 1], topped[d, 1]], axis=1),
            ],
            axis=0,
        )
        y = matmul3(mats[0], mats[1], *split(x))
        y = jnp.concatenate(
            [
                jnp.concatenate([y[:128, :128], y[128:, :128]], axis=1),
                jnp.concatenate([y[:128, 128:], y[128:, 128:]], axis=1),
            ],
            axis=0,
        )
        z = matmul3(*split(y), mats[2], mats[3])
        for k in range(2 * per_chunk):
            p = 2 * per_chunk * pair + k
            rows = slice(piece_rows * k, piece_rows * (k + 1))
            stage[0, p, 0] = z[rows, :128]
            stage[0, p, 1] = z[rows, 128:]
            launch(p, 0)

    coefs = {}
    for b in bits:
        g = gate(local_bits + b)
        one = where_to[b][0] == 1
        coefs[b] = (
            jnp.where(one, g[3], g[0]),
            jnp.where(one, g[7], g[4]),
            jnp.where(one, g[2], g[1]),
            jnp.where(one, g[6], g[5]),
        )

    def finish(p, step):
        copies[p, step].wait()
        cr, ci, dr, di = coefs[orders[p][step]]
        xr, xi = stage[step, p, 0], stage[step, p, 1]
        yr, yi = recv[step, p, 0], recv[step, p, 1]
        zr = (cr * xr - ci * xi) + (dr * yr - di * yi)
        zi = (cr * xi + ci * xr) + (dr * yi + di * yr)
        if step + 1 < len(bits):
            stage[step + 1, p, 0] = zr
            stage[step + 1, p, 1] = zi
            launch(p, step + 1)
        else:
            base = 2 * piece_rows * p
            out_ref[pl.ds(base, piece_rows, stride=2), :] = zr
            out_ref[pl.ds(base + 1, piece_rows, stride=2), :] = zi
            at = pl.ds(base, 2 * piece_rows)
            store = pltpu.make_async_copy(out_ref.at[at], out_hbm.at[at], out_sem.at[p])
            store.start()
            stores.append(store)

    lane = lax.broadcasted_iota(jnp.int32, (8, 128), 1)
    within = lax.broadcasted_iota(jnp.int32, (8, 128), 0) * 128 + lane

    def stat_step(j):
        src, dst = j % 2, (j + 1) % 2
        layer = j // slots
        t = damp[layer, j % slots]
        g = [tab[8 * layer + e, t] for e in range(8)]
        mask, lane_move, sub_move, tile_move = [damp[layers * (1 + m) + layer, j % slots] for m in range(4)]
        lane_up, sub_up = (128 - lane_move) & 127, (8 - sub_move) & 7
        lane_low = (within & lane_move) == 0
        sub_low = (within & (sub_move << 7)) == 0

        def meet(v):
            v = jnp.where(lane_low, pltpu.roll(v, lane_up, 1), pltpu.roll(v, lane_move, 1))
            return jnp.where(sub_low, pltpu.roll(v, sub_up, 0), pltpu.roll(v, sub_move, 0))

        def body(k, acc):
            for u in range(8):
                i = k * 8 + u
                other = i + tile_move - 2 * (i & tile_move)
                xr, xi = planes[src, 0, i], planes[src, 1, i]
                yr, yi = meet(planes[src, 0, other]), meet(planes[src, 1, other])
                bit = ((within + i * 1024) & mask) != 0
                cr, ci = jnp.where(bit, g[3], g[0]), jnp.where(bit, g[7], g[4])
                dr, di = jnp.where(bit, g[2], g[1]), jnp.where(bit, g[6], g[5])
                zr = (cr * xr - ci * xi) + (dr * yr - di * yi)
                zi = (cr * xi + ci * xr) + (dr * yi + di * yr)
                planes[dst, 0, i] = zr
                planes[dst, 1, i] = zi
                acc = acc + (zr * zr + zi * zi)
            return acc

        acc = lax.fori_loop(0, tiles // 8, body, jnp.zeros((8, 128), jnp.float32))
        stats[0, j + 1:j + 2, :] = jnp.sum(acc, axis=0, keepdims=True)

    stat_copies = {}

    def stat_launch(k):
        copy = pltpu.make_async_remote_copy(
            src_ref=stats.at[k],
            dst_ref=stat_recv.at[k],
            send_sem=stat_send.at[k],
            recv_sem=stat_got.at[k],
            device_id=where_to[bits[k]][1],
            device_id_type=MESH,
        )
        copy.start()
        stat_copies[k] = copy

    def stat_finish(k):
        stat_copies[k].wait()
        stats[k + 1] = stats[k] + stat_recv[k]

    def totals():
        summed = jnp.sum(stats[len(bits)], axis=1, keepdims=True) * (1.0 / cfg["whole"])
        factor = jnp.ones((1, 1), jnp.float32)
        info_ref[...] = jnp.zeros_like(info_ref)
        for j in range(layers * slots):
            before = summed[j:j + 1] * factor * factor
            after = summed[j + 1:j + 2] * factor * factor
            info_ref[j:j + 1, :] = jnp.broadcast_to(after / before, (1, 128))
            factor = factor * lax.rsqrt(after + epsilon)
        info_ref[layers * slots:layers * slots + 1, :] = jnp.broadcast_to(factor, (1, 128))

    jobs = [functools.partial(stat_step, j) for j in range(layers * slots)]
    gap = max(1, len(events) // (len(bits) + 2))
    done = 0
    for n, (p, step) in enumerate(events):
        if n < len(jobs):
            jobs[n]()
        finish(p, step)
        if n + 1 >= max(gap * (done + 1), len(jobs)) and done <= len(bits):
            if done > 0:
                stat_finish(done - 1)
            if done < len(bits):
                stat_launch(done)
            else:
                totals()
            done += 1
    assert done == len(bits) + 1
    for store in stores:
        store.wait()


def on_device(initial_state, gate_angles, damp_qubits, kraus_branch, damping):
    local_amps = initial_state.shape[1]
    local_bits = local_amps.bit_length() - 1
    hi, lo = lax.axis_size("hi"), lax.axis_size("lo")
    lo_bits, hi_bits = lo.bit_length() - 1, hi.bit_length() - 1
    bits = list(range(lo_bits + hi_bits))
    rows = local_amps >> LANE_BITS
    pieces = 16
    piece_rows = rows // pieces
    orders, events = plan(bits, [b for b in (1, 2) if b in bits], pieces)
    layers, slots = damp_qubits.shape
    cfg = dict(
        lo_bits=lo_bits, bits=bits, tiles=rows // 8, pieces=pieces, piece_rows=piece_rows,
        local_bits=local_bits, layers=layers, slots=slots, orders=orders, events=events,
        whole=float(local_amps * hi * lo),
    )
    mask = jnp.left_shift(jnp.int32(1), damp_qubits)
    moves = jnp.concatenate([damp_qubits, mask, mask & 127, (mask >> 7) & 7, mask >> 10])
    tab = tables(gate_angles, damp_qubits, kraus_branch, damping)
    x = initial_state.reshape(2, rows, 128).transpose(1, 0, 2).reshape(2 * rows, 128)
    count = len(bits)
    stat_rows = -(-(layers * slots + 1) // 8) * 8
    vmem = pl.BlockSpec(memory_space=pltpu.VMEM)
    whole = pl.BlockSpec(memory_space=pl.ANY)
    smem = pl.BlockSpec(memory_space=pltpu.SMEM)
    out, info = pl.pallas_call(
        functools.partial(kernel, cfg),
        out_shape=(
            jax.ShapeDtypeStruct((2 * rows, 128), jnp.float32),
            jax.ShapeDtypeStruct((stat_rows, 128), jnp.float32),
        ),
        in_specs=[smem, smem, whole],
        out_specs=(whole, vmem),
        scratch_shapes=[
            pltpu.VMEM((2 * rows + 8, 128), jnp.float32),
            pltpu.VMEM((2 * rows + 8, 128), jnp.float32),
            pltpu.VMEM((2, 2, rows // 8, 8, 128), jnp.float32),
            pltpu.VMEM((rows // 128, 2, 128, 128), jnp.float32),
            pltpu.VMEM((count, pieces, 2, piece_rows, 128), jnp.float32),
            pltpu.VMEM((count, pieces, 2, piece_rows, 128), jnp.float32),
            pltpu.VMEM((4, 256, 256), jnp.bfloat16),
            pltpu.VMEM((count + 1, stat_rows, 128), jnp.float32),
            pltpu.VMEM((count, stat_rows, 128), jnp.float32),
            pltpu.SemaphoreType.DMA((count, pieces)),
            pltpu.SemaphoreType.DMA((count, pieces)),
            pltpu.SemaphoreType.DMA((count,)),
            pltpu.SemaphoreType.DMA((count,)),
            pltpu.SemaphoreType.DMA,
            pltpu.SemaphoreType.DMA((pieces,)),
        ],
        compiler_params=pltpu.CompilerParams(
            collective_id=0, has_side_effects=True, vmem_limit_bytes=56 * 1024 * 1024
        ),
    )(tab, moves, x)
    amplitudes = out * info[layers * slots, 0]
    amplitudes = amplitudes.reshape(rows, 2, 128).transpose(1, 0, 2).reshape(2, local_amps)
    weights = info[:layers * slots, 0].reshape(layers, slots)
    return (amplitudes, weights)


def solution(mesh):
    in_specs = (P(None, ("hi", "lo")), P(), P(), P(), P())
    out_specs = (P(None, ("hi", "lo")), P())
    return jax.shard_map(
        on_device, mesh=mesh, in_specs=in_specs, out_specs=out_specs, check_vma=False
    )
```

profile of v0, /device:TPU:0, one launch (start us, length us, event | category | flops | bytes accessed | tf_op | source)
XLA Modules:
  0.0 159.3 jit_solution(13285017459085524384)
XLA Ops:
  0.6 0.0 copy-start.2
  0.6 0.7 copy-done.2
  1.3 0.6 fusion.12
  6.9 0.0 copy-start.3
  6.9 0.7 copy-done.3
  7.6 0.7 fusion.11
  18.9 0.0 copy-start
  18.9 0.7 copy-done
  19.6 0.7 fusion.10
  20.3 0.0 copy-start.1
  20.3 0.7 copy-done.1
  21.0 5.2 %multiply_add_fusion = (f32[1,22]{1,0:T(1,128)S(1)}, f32[1,22]{1,0:T(1,128)S(1)}, f32[1,22]{1,0:T(1,128)S(1)}, f32[1,22]{1,0:T(1,128)S(1)}, f32[1,22]{1,0:T(1,12...) fusion(f32[2,3,22]{2,0,1:T(2,128)S(1)} %copy-done.1, ...), kind=kLoop, calls=%fused_computation.22 | loop fusion | flops 1672 | bytes 1944 | tf_op jit(solution)/shard_map/add | solution.py:56
  26.2 2.6 %multiply_add_fusion.2 = (f32[1,22]{1,0:T(1,128)S(1)}, f32[1,22]{1,0:T(1,128)S(1)}, f32[1,22]{1,0:T(1,128)S(1)}) fusion(f32[1,22]{1,0:T(1,128)S(1)} %get-tuple-element.8, f32[1,22]{1,0:T(1,128)S(1)} %get-tuple-element.7, f32[]{:T(128)} %bitcast.29, s32[]{:T(128)} %bitcast.28, f32[]{:T(128)} %bitcast.27, s32[]{:T(128)} %bitcast.26, f32[]{:T(128)} %bitcast.25, ...), kind=kLoop, calls=%fused_computation.24 | loop fusion | flops 330 | bytes 488 | tf_op jit(solution)/shard_map/add | solution.py:56
  28.8 0.1 multiply_add_fusion.1
  28.9 0.1 multiply_add_fusion.8
  29.0 1.2 stack.2.tab
  30.2 1.2 concatenate.3.damp
  31.4 123.0 %shard_map.68 = (f32[2048,128]{1,0:T(8,128)}, f32[16,128]{1,0:T(8,128)}) custom-call(f32[16,22]{1,0:T(8,128)} %stack.2.tab, s32[10,4]{1,0:T(8,128)} %concatenate.3.damp, f32[2048,128]{1,0:T(8,128)} %bitcast.240), custom_call_target="tpu_custom_call" | custom-call | tf_op jit(solution)/shard_map/pallas_call | solution.py:414
  154.4 1.2 slice.206
  155.6 0.0 copy-start.4
  155.6 2.9 %broadcast_multiply_fusion = f32[2048,128]{1,0:T(8,128)} fusion(f32[2048,128]{1,0:T(8,128)} %get-tuple-element.4, f32[]{:T(128)} %bitcast.47), kind=kLoop, calls=%fused_computation | loop fusion | flops 262144 | bytes 2097156 | tf_op jit(solution)/shard_map/mul | solution.py:443
  158.5 0.0 copy-done.4
  158.5 0.1 slice_reduce_fusion
  158.6 0.6 reshape_squeeze.3
  (2 shorter events, 0.0 us)
Async XLA Ops:
  0.6 0.7 copy-start.2
  6.9 0.7 copy-start.3
  18.9 0.7 copy-start
  20.3 0.7 copy-start.1
  155.6 2.9 %copy-start.4 = (f32[16,128]{1,0:T(8,128)S(1)}, f32[16,128]{1,0:T(8,128)}, u32[]{:S(2)}) copy-start(f32[16,128]{1,0:T(8,128)} %get-tuple-element.5) | copy-start | bytes 24580
where the time goes:
time: 160 us; the launch traced here: 159 us
  Pallas kernels  123 us (77%)
  between operations  16.3 us (10%)
  other arithmetic  10.9 us (7%)
  local copies, waits for them, and re-layouts  9.05 us (6%)
    pallas_call x1, Pallas kernels, on_device(): pl.pallas_call(functools.partial(kernel, cfg), out_shape=(jax.ShapeDtypeS...  123 us
    add x4, other arithmetic, real_times(): imag.append(left[2 * row] * ri[col] + left[2 * row + 1] * ri[2 + col])  7.91 us

commit v1 on v0

--- a/solution.py
+++ b/solution.py
@@ -13,14 +13,23 @@
 MESH = pl.DeviceIdType.MESH
 
 
-def gate_entries(angles):
-    half_theta = angles[1] * 0.5
-    cosine = jnp.cos(half_theta)
-    sine = jnp.sin(half_theta)
-    summed = (angles[0] + angles[2]) * 0.5
-    differ = (angles[0] - angles[2]) * 0.5
-    cos_sum, sin_sum = jnp.cos(summed), jnp.sin(summed)
-    cos_dif, sin_dif = jnp.cos(differ), jnp.sin(differ)
+def sine_cosine(angle):
+    half = angle * 0.5
+    square = half * half
+    sine = 1.0 / 6227020800.0
+    cosine = -1.0 / 87178291200.0
+    for term in (-1.0 / 39916800.0, 1.0 / 362880.0, -1.0 / 5040.0, 1.0 / 120.0, -1.0 / 6.0, 1.0):
+        sine = sine * square + term
+    for term in (1.0 / 479001600.0, -1.0 / 3628800.0, 1.0 / 40320.0, -1.0 / 720.0, 1.0 / 24.0, -0.5, 1.0):
+        cosine = cosine * square + term
+    sine = sine * half
+    return (2.0 * sine * cosine, 1.0 - 2.0 * sine * sine)
+
+
+def gate_entries(a, b, c):
+    sine, cosine = sine_cosine(b * 0.5)
+    sin_sum, cos_sum = sine_cosine((a + c) * 0.5)
+    sin_dif, cos_dif = sine_cosine((a - c) * 0.5)
     real = [cos_sum * cosine, -cos_dif * sine, cos_dif * sine, cos_sum * cosine]
     imag = [-sin_sum * cosine, sin_dif * sine, sin_dif * sine, sin_sum * cosine]
     return (real, imag)
@@ -57,37 +66,38 @@
     return (real, imag)
 
 
-def kraus_entries(qubits, targets, branches, rates):
-    ids = lax.iota(jnp.int32, qubits)
-    one = jnp.ones((qubits,), jnp.float32)
-    zero = jnp.zeros((qubits,), jnp.float32)
+def kraus_entries(shape, targets, branches, rates):
+    ids = lax.broadcasted_iota(jnp.int32, shape, 1)
+    one = jnp.ones(shape, jnp.float32)
+    zero = jnp.zeros(shape, jnp.float32)
     entries = [one, zero, zero, one]
-    for slot in range(targets.shape[0]):
-        here = ids == targets[slot]
-        jump = branches[slot] == 1
-        keep = jnp.sqrt(1.0 - rates[slot])
-        drop = jnp.sqrt(rates[slot])
+    for target, branch, rate in zip(targets, branches, rates):
+        here = ids == target
+        jump = jnp.full(shape, branch, jnp.int32) == 1
+        rate = jnp.full(shape, rate, jnp.float32)
         values = [
-            jnp.where(jump, 0.0, 1.0),
-            jnp.where(jump, drop, 0.0),
-            0.0,
-            jnp.where(jump, 0.0, keep),
+            jnp.where(jump, zero, one),
+            jnp.where(jump, jnp.sqrt(rate), zero),
+            zero,
+            jnp.where(jump, zero, jnp.sqrt(1.0 - rate)),
         ]
         entries = [jnp.where(here, v, e) for v, e in zip(values, entries)]
     return entries
 
 
-def tables(gate_angles, damp_qubits, kraus_branch, damping):
-    layers, _, qubits = gate_angles.shape
+def tables(angles, targets, branches, rates):
+    layers, _, qubits = angles.shape
+    slots = targets.shape[1]
     rows = []
     total = None
     for layer in range(layers):
-        gates = gate_entries(gate_angles[layer])
+        gates = gate_entries(*[angles[layer, k:k + 1, :] for k in range(3)])
         total = gates if total is None else product(gates, total)
-        kraus = kraus_entries(qubits, damp_qubits[layer], kraus_branch[layer], damping[layer])
+        picked = [[ref[layer, slot] for slot in range(slots)] for ref in (targets, branches, rates)]
+        kraus = kraus_entries((1, qubits), *picked)
         total = real_times(kraus, total)
         rows += total[0] + total[1]
-    return jnp.stack(rows)
+    return rows
 
 
 def plan(bits, heavy, pieces):
@@ -131,8 +141,9 @@
     return dot(a_high, b_high) + (dot(a_high, b_low) + dot(a_low, b_high))
 
 
-def kernel(cfg, tab, damp, x_hbm, out_hbm, info_ref, x_ref, out_ref, planes, topped, stage, recv, mats,
-           stats, stat_recv, send_sem, recv_sem, stat_send, stat_got, in_sem, out_sem):
+def kernel(cfg, angles, damp, branches, rates, x_hbm, out_hbm, info_ref, x_ref, out_ref, planes_a, planes_b, topped, stage, recv, mats,
+           stats, stat_recv, send_sem, recv_sem, stat_send, stat_got, in_sem, out_sem,
+           tab_rows, tab, tab_sem):
     lo_bits, bits = cfg["lo_bits"], cfg["bits"]
     tiles, pieces, piece_rows = cfg["tiles"], cfg["pieces"], cfg["piece_rows"]
     local_bits, layers, slots = cfg["local_bits"], cfg["layers"], cfg["slots"]
@@ -154,6 +165,13 @@
     barrier = pltpu.get_barrier_semaphore()
     for b in bits:
         pl.semaphore_signal(barrier, inc=1, device_id=where_to[b][1], device_id_type=MESH)
+
+    tab_rows[...] = jnp.zeros_like(tab_rows)
+    for n, row in enumerate(tables(angles, damp, branches, rates)):
+        tab_rows[n:n + 1, :angles.shape[2]] = row
+    share = pltpu.make_async_copy(tab_rows, tab, tab_sem)
+    share.start()
+    share.wait()
 
     def gate(q):
         return [tab[last + e, q] for e in range(8)]
@@ -194,8 +212,8 @@
             base = pl.multiple_of((c * 16 + i) * 16, 16)
             re = x_ref[pl.ds(base, 8, stride=2), :]
             im = x_ref[pl.ds(base + 1, 8, stride=2), :]
-            planes[0, 0, c * 16 + i] = re
-            planes[0, 1, c * 16 + i] = im
+            planes_a[0, c * 16 + i] = re
+            planes_a[1, c * 16 + i] = im
             acc = acc + (re * re + im * im)
             vals.append((re, im))
         for n in range(top_bits):
@@ -304,38 +322,64 @@
     lane = lax.broadcasted_iota(jnp.int32, (8, 128), 1)
     within = lax.broadcasted_iota(jnp.int32, (8, 128), 0) * 128 + lane
 
-    def stat_step(j):
-        src, dst = j % 2, (j + 1) % 2
+    carry = {}
+    parts, batch = cfg["parts"], cfg["batch"]
+
+    def stat_step(j, part):
+        src, dst = (planes_a, planes_b) if j % 2 == 0 else (planes_b, planes_a)
         layer = j // slots
         t = damp[layer, j % slots]
         g = [tab[8 * layer + e, t] for e in range(8)]
-        mask, lane_move, sub_move, tile_move = [damp[layers * (1 + m) + layer, j % slots] for m in range(4)]
+
+        def power(first, end, unit):
+            value = jnp.int32(0)
+            for n in range(first, end):
+                value = jnp.where(t == n, jnp.int32(1 << (n - unit)), value)
+            return value
+
+        mask = power(0, local_bits, 0)
+        lane_move, sub_move = power(0, 7, 0), power(7, 10, 7)
+        tile_move = power(10, local_bits, 10)
         lane_up, sub_up = (128 - lane_move) & 127, (8 - sub_move) & 7
         lane_low = (within & lane_move) == 0
-        sub_low = (within & (sub_move << 7)) == 0
+        sub_low = (within & (sub_move * 128)) == 0
+        final = j + 1 == layers * slots
 
         def meet(v):
             v = jnp.where(lane_low, pltpu.roll(v, lane_up, 1), pltpu.roll(v, lane_move, 1))
             return jnp.where(sub_low, pltpu.roll(v, sub_up, 0), pltpu.roll(v, sub_move, 0))
 
         def body(k, acc):
-            for u in range(8):
-                i = k * 8 + u
-                other = i + tile_move - 2 * (i & tile_move)
-                xr, xi = planes[src, 0, i], planes[src, 1, i]
-                yr, yi = meet(planes[src, 0, other]), meet(planes[src, 1, other])
+            ids = [k * batch + u for u in range(batch)]
+            others = [i + tile_move - 2 * (i & tile_move) for i in ids]
+            xs = [(src[0, i], src[1, i]) for i in ids]
+            ys = [(src[0, o], src[1, o]) for o in others]
+            ys = [(meet(yr), meet(yi)) for yr, yi in ys]
+            zs = []
+            for i, (xr, xi), (yr, yi) in zip(ids, xs, ys):
                 bit = ((within + i * 1024) & mask) != 0
                 cr, ci = jnp.where(bit, g[3], g[0]), jnp.where(bit, g[7], g[4])
                 dr, di = jnp.where(bit, g[2], g[1]), jnp.where(bit, g[6], g[5])
                 zr = (cr * xr - ci * xi) + (dr * yr - di * yi)
                 zi = (cr * xi + ci * xr) + (dr * yi + di * yr)
-                planes[dst, 0, i] = zr
-                planes[dst, 1, i] = zi
-                acc = acc + (zr * zr + zi * zi)
-            return acc
-
-        acc = lax.fori_loop(0, tiles // 8, body, jnp.zeros((8, 128), jnp.float32))
-        stats[0, j + 1:j + 2, :] = jnp.sum(acc, axis=0, keepdims=True)
+                zs.append((zr, zi))
+            for i, (zr, zi) in zip(ids, zs):
+                if not final:
+                    dst[0, i] = zr
+                    dst[1, i] = zi
+            squares = [zr * zr + zi * zi for zr, zi in zs]
+            while len(squares) > 1:
+                squares = [u + v for u, v in zip(squares[::2], squares[1::2])]
+            return acc + squares[0]
+
+        steps = tiles // batch // parts
+        acc = carry.pop(j, None)
+        acc = jnp.zeros((8, 128), jnp.float32) if acc is None else acc
+        acc = lax.fori_loop(part * steps, (part + 1) * steps, body, acc)
+        if part + 1 < parts:
+            carry[j] = acc
+        else:
+            stats[0, j + 1:j + 2, :] = jnp.sum(acc, axis=0, keepdims=True)
 
     stat_copies = {}
 
@@ -366,14 +410,16 @@
             factor = factor * lax.rsqrt(after + epsilon)
         info_ref[layers * slots:layers * slots + 1, :] = jnp.broadcast_to(factor, (1, 128))
 
-    jobs = [functools.partial(stat_step, j) for j in range(layers * slots)]
-    gap = max(1, len(events) // (len(bits) + 2))
+    jobs = [functools.partial(stat_step, j, part) for j in range(layers * slots) for part in range(parts)]
+    per = -(-len(jobs) // max(1, len(events) // 3))
+    ready = -(-len(jobs) // per)
+    gap = max(1, (len(events) - ready) // (len(bits) + 1))
     done = 0
     for n, (p, step) in enumerate(events):
-        if n < len(jobs):
-            jobs[n]()
+        for job in jobs[n * per:(n + 1) * per]:
+            job()
         finish(p, step)
-        if n + 1 >= max(gap * (done + 1), len(jobs)) and done <= len(bits):
+        if n + 1 >= ready + gap * done and done <= len(bits):
             if done > 0:
                 stat_finish(done - 1)
             if done < len(bits):
@@ -398,13 +444,11 @@
     orders, events = plan(bits, [b for b in (1, 2) if b in bits], pieces)
     layers, slots = damp_qubits.shape
     cfg = dict(
+        parts=2, batch=8,
         lo_bits=lo_bits, bits=bits, tiles=rows // 8, pieces=pieces, piece_rows=piece_rows,
         local_bits=local_bits, layers=layers, slots=slots, orders=orders, events=events,
         whole=float(local_amps * hi * lo),
     )
-    mask = jnp.left_shift(jnp.int32(1), damp_qubits)
-    moves = jnp.concatenate([damp_qubits, mask, mask & 127, (mask >> 7) & 7, mask >> 10])
-    tab = tables(gate_angles, damp_qubits, kraus_branch, damping)
     x = initial_state.reshape(2, rows, 128).transpose(1, 0, 2).reshape(2 * rows, 128)
     count = len(bits)
     stat_rows = -(-(layers * slots + 1) // 8) * 8
@@ -417,12 +461,13 @@
             jax.ShapeDtypeStruct((2 * rows, 128), jnp.float32),
             jax.ShapeDtypeStruct((stat_rows, 128), jnp.float32),
         ),
-        in_specs=[smem, smem, whole],
+        in_specs=[vmem, smem, smem, smem, whole],
         out_specs=(whole, vmem),
         scratch_shapes=[
             pltpu.VMEM((2 * rows + 8, 128), jnp.float32),
             pltpu.VMEM((2 * rows + 8, 128), jnp.float32),
-            pltpu.VMEM((2, 2, rows // 8, 8, 128), jnp.float32),
+            pltpu.VMEM((2, rows // 8, 8, 128), jnp.float32),
+            pltpu.VMEM((2, rows // 8, 8, 128), jnp.float32),
             pltpu.VMEM((rows // 128, 2, 128, 128), jnp.float32),
             pltpu.VMEM((count, pieces, 2, piece_rows, 128), jnp.float32),
             pltpu.VMEM((count, pieces, 2, piece_rows, 128), jnp.float32),
@@ -435,11 +480,14 @@
             pltpu.SemaphoreType.DMA((count,)),
             pltpu.SemaphoreType.DMA,
             pltpu.SemaphoreType.DMA((pieces,)),
+            pltpu.VMEM((8 * layers, 128), jnp.float32),
+            pltpu.SMEM((8 * layers, 128), jnp.float32),
+            pltpu.SemaphoreType.DMA,
         ],
         compiler_params=pltpu.CompilerParams(
             collective_id=0, has_side_effects=True, vmem_limit_bytes=56 * 1024 * 1024
         ),
-    )(tab, moves, x)
+    )(gate_angles, damp_qubits, kraus_branch, damping, x)
     amplitudes = out * info[layers * slots, 0]
     amplitudes = amplitudes.reshape(rows, 2, 128).transpose(1, 0, 2).reshape(2, local_amps)
     weights = info[:layers * slots, 0].reshape(layers, slots)

time: 160 us -> 65 us (0.41)
  Pallas kernels: 123 us -> 57.9 us
  between operations: 16.3 us -> 0.64 us
  other arithmetic: 10.9 us -> 2.92 us
  local copies, waits for them, and re-layouts: 9.05 us -> 3.23 us
    pallas_call x1, Pallas kernels: 123 us -> 57.9 us  [on_device(): pl.pallas_call(functools.partial(kernel, cfg), out_shape=(jax.ShapeDtypeS...]
    add x5 -> x0, other arithmetic: 7.98 us -> none  [the longest x4 7.91 us: real_times(): imag.append(left[2 * row] * ri[col] + left[2 * row + 1] * ri[2 + col])]
    slice x3 -> x0, local copies, waits for them, and re-layouts: 1.96 us -> none  [the longest x1 0.68 us: kraus_entries(): here = ids == targets[slot]]
where the time goes in v1:
time: 65 us; the launch traced here: 64.7 us
  Pallas kernels  57.9 us (89%)
  local copies, waits for them, and re-layouts  3.23 us (5%)
  other arithmetic  2.92 us (4%)
    pallas_call x1, Pallas kernels, on_device(): pl.pallas_call(functools.partial(kernel, cfg), out_shape=(jax.ShapeDtypeS...  57.9 us
    mul x1, other arithmetic, on_device(): amplitudes = out * info[layers * slots, 0]  2.92 us

profile of v1, /device:TPU:0, one launch (start us, length us, event | category | flops | bytes accessed | tf_op | source)
XLA Modules:
  0.0 64.7 jit_solution(3595230505482086134)
XLA Ops:
  0.6 1.3 %copy.11.angles = f32[2,3,22]{2,1,0:T(4,128)} copy(f32[2,3,22]{2,0,1:T(2,128)} %param.6) | data formatting | bytes 1056 | tf_op args[1]
  1.9 57.9 %shard_map.68 = (f32[2048,128]{1,0:T(8,128)}, f32[16,128]{1,0:T(8,128)}) custom-call(f32[2,3,22]{2,1,0:T(4,128)} %copy.11.angles, s32[2,4]{1,0:T(2,128)} %damp.1, s32[2,4]{1,0:T(2,128)} %branches.1, f32[2,4]{1,0:T(2,128)} %rates.1, f32[2048,128]{1,0:T(8,128)} %bitcast.12), custom_call_target="tpu_custom_call" | custom-call | tf_op jit(solution)/shard_map/pallas_call | solution.py:458
  59.8 1.2 %slice.6 = f32[1,1]{1,0:T(1,128)} slice(f32[16,128]{1,0:T(8,128)} %get-tuple-element.5), slice={[8:9], [0:1]} | slice | bytes 8 | tf_op jit(solution)/shard_map/slice | solution.py:491
  61.0 0.0 copy-start
  61.0 2.9 %broadcast_multiply_fusion = f32[2048,128]{1,0:T(8,128)} fusion(f32[2048,128]{1,0:T(8,128)} %get-tuple-element.4, f32[]{:T(128)} %bitcast.3), kind=kLoop, calls=%fused_computation | loop fusion | flops 262144 | bytes 2097156 | tf_op jit(solution)/shard_map/mul | solution.py:491
  63.9 0.0 copy-done
  63.9 0.1 slice_reduce_fusion
  64.0 0.6 %reshape_squeeze.3 = f32[2,4]{1,0:T(2,128)} reshape(f32[8]{0:T(128)S(1)} %slice_reduce_fusion) | data formatting | bytes 64 | tf_op jit(solution)/shard_map/reshape;squeeze | solution.py:493
Async XLA Ops:
  61.0 2.9 %copy-start = (f32[16,128]{1,0:T(8,128)S(1)}, f32[16,128]{1,0:T(8,128)}, u32[]{:S(2)}) copy-start(f32[16,128]{1,0:T(8,128)} %get-tuple-element.5) | copy-start | bytes 24580

commit v2 on v1

--- a/solution.py
+++ b/solution.py
@@ -86,12 +86,12 @@
 
 
 def tables(angles, targets, branches, rates):
-    layers, _, qubits = angles.shape
+    _, layers, qubits = angles.shape
     slots = targets.shape[1]
     rows = []
     total = None
     for layer in range(layers):
-        gates = gate_entries(*[angles[layer, k:k + 1, :] for k in range(3)])
+        gates = gate_entries(*[angles[k, layer:layer + 1, :] for k in range(3)])
         total = gates if total is None else product(gates, total)
         picked = [[ref[layer, slot] for slot in range(slots)] for ref in (targets, branches, rates)]
         kraus = kraus_entries((1, qubits), *picked)
@@ -403,12 +403,17 @@
         summed = jnp.sum(stats[len(bits)], axis=1, keepdims=True) * (1.0 / cfg["whole"])
         factor = jnp.ones((1, 1), jnp.float32)
         info_ref[...] = jnp.zeros_like(info_ref)
-        for j in range(layers * slots):
-            before = summed[j:j + 1] * factor * factor
-            after = summed[j + 1:j + 2] * factor * factor
-            info_ref[j:j + 1, :] = jnp.broadcast_to(after / before, (1, 128))
-            factor = factor * lax.rsqrt(after + epsilon)
-        info_ref[layers * slots:layers * slots + 1, :] = jnp.broadcast_to(factor, (1, 128))
+        line = lax.broadcasted_iota(jnp.int32, (1, 128), 1)
+        for layer in range(layers):
+            weights = jnp.zeros((1, 128), jnp.float32)
+            for slot in range(slots):
+                j = layer * slots + slot
+                before = summed[j:j + 1] * factor * factor
+                after = summed[j + 1:j + 2] * factor * factor
+                weights = jnp.where(line == slot, after / before, weights)
+                factor = factor * lax.rsqrt(after + epsilon)
+            info_ref[layer:layer + 1, :] = weights
+        info_ref[layers:layers + 1, :] = jnp.broadcast_to(factor, (1, 128))
 
     jobs = [functools.partial(stat_step, j, part) for j in range(layers * slots) for part in range(parts)]
     per = -(-len(jobs) // max(1, len(events) // 3))
@@ -428,6 +433,27 @@
                 totals()
             done += 1
     assert done == len(bits) + 1
+    for store in stores:
+        store.wait()
+
+
+def scale_kernel(blocks, info, x_hbm, out_hbm, weights, held, scaled, in_sem, out_sem):
+    layers, slots = weights.shape
+    size = held.shape[0] // blocks
+    loads, stores = [], []
+    for n in range(blocks):
+        at = pl.ds(n * size, size)
+        loads.append(pltpu.make_async_copy(x_hbm.at[at], held.at[at], in_sem.at[n]))
+        stores.append(pltpu.make_async_copy(scaled.at[at], out_hbm.at[at], out_sem.at[n]))
+    for load in loads:
+        load.start()
+    weights[...] = info[:layers, :slots]
+    factor = info[layers:layers + 1, :]
+    for n in range(blocks):
+        at = pl.ds(n * size, size)
+        loads[n].wait()
+        scaled[at, :] = held[at, :] * factor
+        stores[n].start()
     for store in stores:
         store.wait()
 
@@ -487,10 +513,24 @@
         compiler_params=pltpu.CompilerParams(
             collective_id=0, has_side_effects=True, vmem_limit_bytes=56 * 1024 * 1024
         ),
-    )(gate_angles, damp_qubits, kraus_branch, damping, x)
-    amplitudes = out * info[layers * slots, 0]
+    )(gate_angles.transpose(1, 0, 2), damp_qubits, kraus_branch, damping, x)
+    blocks = 8
+    amplitudes, weights = pl.pallas_call(
+        functools.partial(scale_kernel, blocks),
+        out_shape=(
+            jax.ShapeDtypeStruct((2 * rows, 128), jnp.float32),
+            jax.ShapeDtypeStruct((layers, slots), jnp.float32),
+        ),
+        in_specs=[vmem, whole],
+        out_specs=(whole, vmem),
+        scratch_shapes=[
+            pltpu.VMEM((2 * rows, 128), jnp.float32),
+            pltpu.VMEM((2 * rows, 128), jnp.float32),
+            pltpu.SemaphoreType.DMA((blocks,)),
+            pltpu.SemaphoreType.DMA((blocks,)),
+        ],
+    )(info, out)
     amplitudes = amplitudes.reshape(rows, 2, 128).transpose(1, 0, 2).reshape(2, local_amps)
-    weights = info[:layers * slots, 0].reshape(layers, slots)
     return (amplitudes, weights)
 
 

time: 65 us -> 62.1 us (0.955)
  Pallas kernels: 57.9 us -> 61.2 us
  local copies, waits for them, and re-layouts: 3.23 us -> 0 us
  other arithmetic: 2.92 us -> 0 us
    pallas_call x0 -> x1, Pallas kernels: none -> 3.35 us  [on_device(): pl.pallas_call(functools.partial(scale_kernel, blocks), out_shape=(jax.Sh...]
    mul x1 -> x0, other arithmetic: 2.92 us -> none  [on_device(): amplitudes = out * info[layers * slots, 0]]
    slice x2 -> x0, local copies, waits for them, and re-layouts: 1.3 us -> none  [the longest x1 1.19 us: on_device(): amplitudes = out * info[layers * slots, 0]]
    unnamed x3 -> x0, local copies, waits for them, and re-layouts: 1.28 us -> none
where the time goes in v2:
time: 62.1 us; the launch traced here: 61.9 us
  Pallas kernels  61.2 us (99%)
  between operations  0.64 us (1%)
    pallas_call x1, Pallas kernels, on_device(): pl.pallas_call(functools.partial(kernel, cfg), out_shape=(jax.ShapeDtypeS...  57.9 us
    pallas_call x1, Pallas kernels, on_device(): pl.pallas_call(functools.partial(scale_kernel, blocks), out_shape=(jax.Sh...  3.35 us

profile of v2, /device:TPU:0, one launch (start us, length us, event | category | flops | bytes accessed | tf_op | source)
XLA Modules:
  0.0 61.9 jit_solution(7641498497970764035)
XLA Ops:
  0.6 57.9 %shard_map.68 = (f32[2048,128]{1,0:T(8,128)}, f32[16,128]{1,0:T(8,128)}) custom-call(f32[3,2,22]{2,1,0:T(2,128)} %bitcast.12, s32[2,4]{1,0:T(2,128)} %damp.1, s32[2,4]{1,0:T(2,128)} %branches.1, f32[2,4]{1,0:T(2,128)} %rates.1, f32[2048,128]{1,0:T(8,128)} %bitcast.11), custom_call_target="tpu_custom_call" | custom-call | tf_op jit(solution)/shard_map/pallas_call | solution.py:484
  58.5 3.4 %shard_map.69 = (f32[2048,128]{1,0:T(8,128)}, f32[2,4]{1,0:T(2,128)}) custom-call(f32[16,128]{1,0:T(8,128)} %get-tuple-element.6.info, f32[2048,128]{1,0:T(8,128)} %get-tuple-element.7.x_hbm), custom_call_target="tpu_custom_call" | custom-call | tf_op jit(solution)/shard_map/pallas_call | solution.py:518
